TPU v7x, 32 devices: a whole 2x2x4 slice. The times are simulated.
32 devices in a mesh: pool: 8 (over z, core), band: 4 (over y, x).
Axes of the slice: x: 2, y: 2, z: 4, core: 2. Of those that a mesh axis runs over, the one named last changes fastest.
Arguments:
- orbitals: float32 [8, 4, 2, 13824], P('pool', 'band'), may hold values from -6 to 6
- kpoints: float32 [8, 3], replicated, may hold values from -0.5 to 0.5
- owner: int32 [1], replicated, may hold values from 0 to 7
Outputs:
- exchange: float32 [8, 4, 2, 13824], P('pool', 'band')
All inputs are finite; a program needn't handle non-finite values.
Results may differ from a plain program's by a relative error of at most 0.0001.
Values sent between devices are 32-bit elements; how exact they have to be, the bound alone decides.
A program may use at most 64 MiB of HBM per device.

v0:
```python
import math
import jax
import jax.numpy as jnp
from jax import lax
from jax.sharding import PartitionSpec as P

NG = 24
mixing = 0.25
kernel_scale = 60.0
screening = 4.0


def frequencies():
    idx = jnp.arange(NG, dtype=jnp.int32)
    return ((idx + NG // 2) % NG - NG // 2).astype(jnp.float32)


def coulomb(dvec):
    freq = frequencies()
    square = (
        (freq[:, None, None] + dvec[0]) ** 2
        + (freq[None, :, None] + dvec[1]) ** 2
        + (freq[None, None, :] + dvec[2]) ** 2
    )
    return (kernel_scale / (square + screening)).reshape(-1)


def dft_matrix(direction, factor):
    idx = jnp.arange(NG, dtype=jnp.int32)
    phase = (idx[:, None] * idx[None, :] % NG).astype(jnp.float32) * (2.0 * math.pi / NG)
    cosine = jnp.cos(phase) * factor
    sine = direction * jnp.sin(phase) * factor
    upper = jnp.concatenate([cosine, -sine], axis=1)
    lower = jnp.concatenate([sine, cosine], axis=1)
    return jnp.concatenate([upper, lower], axis=0)


def transform(field, matrix):
    batch = field.shape[0]
    work = field.reshape(batch, 2 * NG, NG * NG)
    for turn in range(3):
        work = jnp.einsum("ij,pjk->pik", matrix, work, precision=lax.Precision.HIGHEST)
        work = (
            work.reshape(batch, 2, NG, NG, NG)
            .transpose(0, 1, 3, 4, 2)
            .reshape(batch, 2 * NG, NG * NG)
        )
    return work.reshape(batch, 2, NG * NG * NG)


def contribution(sources, resident, kernel, forward, inverse):
    count_s = sources.shape[0]
    count_r = resident.shape[0]
    src_re = sources[:, 0][:, None, :]
    src_im = sources[:, 1][:, None, :]
    res_re = resident[:, 0][None, :, :]
    res_im = resident[:, 1][None, :, :]
    dens_re = src_re * res_re + src_im * res_im
    dens_im = src_re * res_im - src_im * res_re
    density = jnp.stack([dens_re, dens_im], axis=2).reshape(count_s * count_r, 2, -1)
    spectrum = transform(density, forward) * kernel
    potential = transform(spectrum, inverse).reshape(count_s, count_r, 2, -1)
    pot_re = potential[:, :, 0]
    pot_im = potential[:, :, 1]
    out_re = -mixing * jnp.sum(src_re * pot_re - src_im * pot_im, axis=0)
    out_im = -mixing * jnp.sum(src_re * pot_im + src_im * pot_re, axis=0)
    return jnp.stack([out_re, out_im], axis=1)


def shards(orbitals, kpoints, owner):
    resident = orbitals[0]
    pool_index = lax.axis_index("pool")
    kvec = lax.dynamic_index_in_dim(kpoints, pool_index, 0, keepdims=False)
    forward = dft_matrix(-1.0, 1.0)
    inverse = dft_matrix(1.0, 1.0 / NG)
    source_k = owner[0]
    qvec = lax.dynamic_index_in_dim(kpoints, source_k, 0, keepdims=False)
    kernel = coulomb(kvec - qvec)
    masked = jnp.where(pool_index == source_k, resident, jnp.zeros_like(resident))
    sources = lax.psum(masked, "pool")
    total = contribution(
        lax.all_gather(sources, "band", axis=0, tiled=True), resident, kernel, forward, inverse
    )
    return total[None]


def solution(mesh):
    placed = (P("pool", "band", None, None), P(), P())
    return jax.shard_map(
        shards, mesh=mesh, in_specs=placed, out_specs=P("pool", "band", None, None), check_vma=False
    )
```

profile of v0, /device:TPU:8, one launch (start us, length us, event | category | flops | bytes accessed | tf_op | source)
XLA Modules:
  0.0 122.1 jit_solution(5851988328339792703)
XLA Ops:
  7.2 1.6 %broadcast_select_fusion = f32[1,2,13824]{2,1,0:T(2,128)} fusion(pred[]{:T(512)S(6)} %eq.8, f32[1,1,2,13824]{3,2,1,0:T(2,128)} %param.3), kind=kLoop, calls=%fused_computation.16 | loop fusion | flops 27648 | bytes 221185 | tf_op jit(solution)/shard_map/jit(_where)/select_n | solution.py:79
  9.0 1.3 %slice_reduce_fusion.1 = (f32[13824]{0:T(1024)S(1)}, f32[13824]{0:T(1024)S(1)}) fusion(f32[1,2,13824]{2,1,0:T(2,128)} %bitcast.81), kind=kLoop, calls=%fused_computation.19 | loop fusion | bytes 221184 | tf_op jit(solution)/shard_map/slice | solution.py:56
  10.3 0.8 dynamic-slice_subtract_fusion
  11.2 0.6 fusion.21
  11.8 0.7 add_multiply_fusion.2
  12.5 1.3 %add_multiply_fusion = (f32[24]{0:T(128)S(1)}, f32[24]{0:T(128)S(1)}) fusion(f32[]{:T(128)} %bitcast.13, f32[]{:T(128)} %bitcast.12), kind=kLoop, calls=%fused_computation.43 | loop fusion | flops 312 | bytes 200 | tf_op jit(solution)/shard_map/integer_pow | solution.py:23
  14.3 50.5 %all-reduce.2.cloned.1.call-done = f32[1,2,13824]{2,1,0:T(2,128)} async-done(((f32[1,2,13824]{2,1,0:T(2,128)}), f32[1,2,13824]{2,1,0:T(2,128)}) %all-reduce.2.cloned.1.call-update) | async-done | bytes 110608 | tf_op jit(solution)/shard_map/psum | solution.py:80
  64.8 10.7 %all_gather.3 = f32[4,2,13824]{2,1,0:T(2,128)S(1)} all-gather(f32[1,2,13824]{2,1,0:T(2,128)} %all-reduce.2.cloned.1.call-done), channel_id=1, replica_groups=mesh['pool'=8,'band'=4] {'band'}, dimensions={0}, use_global_device_ids=true | all-gather | bytes 552960 | tf_op jit(solution)/shard_map/all_gather | solution.py:82
  75.9 1.4 %maximum_reduce_fusion = f32[4,2,13824]{2,1,0:T(2,128)S(1)} fusion(f32[4,1,1,13824]{3,1,2,0:T(1,128)S(1)} %get-tuple-element.10, f32[4,1,1,13824]{3,1,2,0:T(1,128)S(1)} %get-tuple-element.9), kind=kLoop, calls=%fused_computation.7 | loop fusion | flops 110592 | bytes 884736 | tf_op jit(solution)/shard_map/stack | solution.py:60
  78.3 0.9 reshape.181
  79.2 2.2 %copy.10 = f32[4,2,24,24,24]{4,3,2,1,0:T(8,128)} copy(f32[4,2,24,24,24]{3,2,4,1,0:T(8,128)S(1)} %bitcast.74) | data formatting | bytes 884736 | tf_op jit(solution)/shard_map/transpose | solution.py:45
  81.4 2.2 %reshape.182 = f32[4,48,576]{2,1,0:T(8,128)S(1)} reshape(f32[4,2,24,24,24]{4,3,2,1,0:T(8,128)} %copy.10) | data formatting | bytes 884736 | tf_op jit(solution)/shard_map/reshape | solution.py:46
  84.2 0.9 reshape.183
  85.1 2.0 %copy.11 = f32[4,2,24,24,24]{4,3,2,1,0:T(8,128)} copy(f32[4,2,24,24,24]{3,2,4,1,0:T(8,128)S(1)} %bitcast.75) | data formatting | bytes 884736 | tf_op jit(solution)/shard_map/transpose | solution.py:45
  87.1 2.2 %reshape.184 = f32[4,48,576]{2,1,0:T(8,128)S(1)} reshape(f32[4,2,24,24,24]{4,3,2,1,0:T(8,128)} %copy.11) | data formatting | bytes 884736 | tf_op jit(solution)/shard_map/reshape | solution.py:46
  89.3 0.6 convolution_bitcast_fusion.3
  89.9 0.9 reshape.185
  90.8 2.0 %copy.12 = f32[4,2,24,24,24]{4,3,2,1,0:T(8,128)} copy(f32[4,2,24,24,24]{3,2,4,1,0:T(8,128)S(1)} %bitcast.76) | data formatting | bytes 884736 | tf_op jit(solution)/shard_map/transpose | solution.py:45
  92.8 2.2 %reshape_reshape.7 = f32[4,48,576]{2,1,0:T(8,128)S(1)} reshape(f32[4,2,24,24,24]{4,3,2,1,0:T(8,128)} %copy.12) | data formatting | bytes 884736 | tf_op jit(solution)/shard_map/reshape;reshape | solution.py:48
  95.7 0.9 reshape.186
  96.6 2.0 %copy.13 = f32[4,2,24,24,24]{4,3,2,1,0:T(8,128)} copy(f32[4,2,24,24,24]{3,2,4,1,0:T(8,128)S(1)} %bitcast.77) | data formatting | bytes 884736 | tf_op jit(solution)/shard_map/transpose | solution.py:45
  98.5 2.2 %reshape.187 = f32[4,48,576]{2,1,0:T(8,128)S(1)} reshape(f32[4,2,24,24,24]{4,3,2,1,0:T(8,128)} %copy.13) | data formatting | bytes 884736 | tf_op jit(solution)/shard_map/reshape | solution.py:46
  100.8 0.6 convolution_bitcast_fusion.1
  101.4 0.9 reshape.188
  102.3 2.0 %copy.14 = f32[4,2,24,24,24]{4,3,2,1,0:T(8,128)} copy(f32[4,2,24,24,24]{3,2,4,1,0:T(8,128)S(1)} %bitcast.78) | data formatting | bytes 884736 | tf_op jit(solution)/shard_map/transpose | solution.py:45
  104.3 2.5 %reshape.189 = f32[4,48,576]{2,1,0:T(8,128)S(1)} reshape(f32[4,2,24,24,24]{4,3,2,1,0:T(8,128)} %copy.14) | data formatting | bytes 884736 | tf_op jit(solution)/shard_map/reshape | solution.py:46
  106.7 0.6 convolution_bitcast_fusion
  107.4 0.9 reshape.190
  108.2 2.0 %copy.15 = f32[4,2,24,24,24]{4,3,2,1,0:T(8,128)} copy(f32[4,2,24,24,24]{3,2,4,1,0:T(8,128)S(1)} %bitcast.79) | data formatting | bytes 884736 | tf_op jit(solution)/shard_map/transpose | solution.py:45
  110.2 3.3 %reshape_reshape_reshape.3 = f32[4,1,2,13824]{3,1,2,0:T(1,128)S(1)} reshape(f32[4,2,24,24,24]{4,3,2,1,0:T(8,128)} %copy.15) | data formatting | bytes 884736 | tf_op jit(solution)/shard_map/reshape;reshape;reshape | solution.py:62
  113.5 0.9 subtract_reduce_fusion
  114.5 0.7 maximum_bitcast_fusion
  (22 shorter events, 3.5 us)
Async XLA Ops:
  6.5 58.3 %all-reduce.2.cloned.1.call-start = ((), (), s32[]{:S(2)}) async-start(), calls=%async_computation | async-start | bytes 221184 | tf_op jit(solution)/shard_map/psum | solution.py:80
Sparse Core Ops, SparseCore 0:
  9.7 55.0 all-reduce.1
where the time goes:
time: 123 us; the launch traced here: 122 us
  waiting for transfers between devices  50.5 us (41%)
  local copies, waits for them, and re-layouts  34.8 us (28%)
  between operations  14.3 us (12%)
  blocking collectives  10.7 us (9%)
  other arithmetic  8.27 us (7%)
  matrix products  3.56 us (3%)
    psum x1, waiting for transfers between devices, shards(): sources = lax.psum(masked, 'pool')  50.5 us
    transpose x6, local copies, waits for them, and re-layouts, transform(): work = work.reshape(batch, 2, NG, NG, NG).transpose(0, 1, 3, 4, 2).reshap...  12 us
    all_gather x1, blocking collectives, shards(): lax.all_gather(sources, 'band', axis=0, tiled=True)  10.7 us
    reshape x4, local copies, waits for them, and re-layouts, transform(): work = work.reshape(batch, 2, NG, NG, NG).transpose(0, 1, 3, 4, 2).reshap...  9.21 us
    reshape x6, local copies, waits for them, and re-layouts, transform(): work.reshape(batch, 2, NG, NG, NG).transpose(0, 1, 3, 4, 2)  5.29 us
    dot_general x6, matrix products, transform(): jnp.einsum('ij,pjk->pik', matrix, work, precision=lax.Precision.HIGHEST)  3.56 us
    another operation x1, local copies, waits for them, and re-layouts, contribution(): potential = transform(spectrum, inverse).reshape(count_s, count_r, 2, -1)  3.31 us
  transfers between devices with their start and end apart: 1, of which 1 were waited for; matrix products, arithmetic and copies ran while one was open for 4% of the time, Pallas kernels for 0%

commit v1 on v0

--- a/solution.py
+++ b/solution.py
@@ -1,3 +1,4 @@
+import functools
 import math
 import jax
 import jax.numpy as jnp
@@ -8,6 +9,24 @@
 mixing = 0.25
 kernel_scale = 60.0
 screening = 4.0
+
+
+def deliver_sample(local_block, axis_id):
+    dev_count = jax.lax.axis_size(axis_id)
+    leaves = [(p, (p + 1) % dev_count) for p in range(dev_count)]
+    log = [(p, (p - 1) % dev_count) for p in range(dev_count)]
+    tall, z = ([local_block], [local_block])
+    for _ in range(dev_count // 2):
+        tall.append(jax.lax.ppermute(tall[-1], axis_id, leaves))
+    for _ in range((dev_count - 1) // 2):
+        z.append(jax.lax.ppermute(z[-1], axis_id, log))
+    kept_arr = jnp.concatenate([*tall[::-1], *z[1:]], axis=0)
+    return jnp.roll(
+        kept_arr, (jax.lax.axis_index(axis_id) - dev_count // 2) * local_block.shape[0], axis=0
+    )
+
+
+pairs_all_play = functools.partial(deliver_sample, axis_id="band")
 
 
 def frequencies():
@@ -78,9 +97,7 @@
     kernel = coulomb(kvec - qvec)
     masked = jnp.where(pool_index == source_k, resident, jnp.zeros_like(resident))
     sources = lax.psum(masked, "pool")
-    total = contribution(
-        lax.all_gather(sources, "band", axis=0, tiled=True), resident, kernel, forward, inverse
-    )
+    total = contribution(pairs_all_play(sources), resident, kernel, forward, inverse)
     return total[None]
 
 

time: 123 us -> 127 us (1.033)
  blocking collectives: 10.7 us -> 0 us
  waiting for transfers between devices: 50.5 us -> 57.8 us
  starting transfers between devices: 0.01 us -> 4.45 us
  local copies, waits for them, and re-layouts: 34.8 us -> 37.2 us
    all_gather x1 -> x0, blocking collectives: 10.7 us -> none  [shards(): lax.all_gather(sources, 'band', axis=0, tiled=True)]
    ppermute x0 -> x3, waiting for transfers between devices: none -> 7.15 us  [the longest x2 6.91 us: deliver_sample(): tall.append(jax.lax.ppermute(tall[-1], axis_id, leaves))]
    ppermute x0 -> x3, starting transfers between devices: none -> 4.45 us  [the longest x1 2.37 us: deliver_sample(): z.append(jax.lax.ppermute(z[-1], axis_id, log))]
    unnamed x0 -> x11, local copies, waits for them, and re-layouts: none -> 2.33 us
  transfers between devices with their start and end apart: 1 -> 4, of which waited for: 1 -> 4; matrix products, arithmetic and copies ran while one was open for 4% -> 5% of each run, Pallas kernels for 0% -> 0%
where the time goes in v1:
time: 127 us; the launch traced here: 126 us
  waiting for transfers between devices  57.8 us (46%)
  local copies, waits for them, and re-layouts  37.2 us (29%)
  between operations  14.4 us (11%)
  other arithmetic  8.31 us (7%)
  starting transfers between devices  4.45 us (4%)
  matrix products  3.57 us (3%)
    psum x1, waiting for transfers between devices, shards(): sources = lax.psum(masked, 'pool')  50.6 us
    transpose x6, local copies, waits for them, and re-layouts, transform(): work = work.reshape(batch, 2, NG, NG, NG).transpose(0, 1, 3, 4, 2).reshap...  12 us
    reshape x4, local copies, waits for them, and re-layouts, transform(): work = work.reshape(batch, 2, NG, NG, NG).transpose(0, 1, 3, 4, 2).reshap...  9.21 us
    ppermute x2, waiting for transfers between devices, deliver_sample(): tall.append(jax.lax.ppermute(tall[-1], axis_id, leaves))  6.91 us
    reshape x6, local copies, waits for them, and re-layouts, transform(): work.reshape(batch, 2, NG, NG, NG).transpose(0, 1, 3, 4, 2)  5.28 us
    dot_general x6, matrix products, transform(): jnp.einsum('ij,pjk->pik', matrix, work, precision=lax.Precision.HIGHEST)  3.57 us
    another operation x1, local copies, waits for them, and re-layouts, contribution(): potential = transform(spectrum, inverse).reshape(count_s, count_r, 2, -1)  3.39 us
  transfers between devices with their start and end apart: 4, of which 4 were waited for; matrix products, arithmetic and copies ran while one was open for 5% of the time, Pallas kernels for 0%

profile of v1, /device:TPU:8, one launch (start us, length us, event | category | flops | bytes accessed | tf_op | source)
XLA Modules:
  0.0 125.8 jit_solution(3084912093021170894)
XLA Ops:
  7.2 1.6 %broadcast_select_fusion = f32[1,2,13824]{2,1,0:T(2,128)} fusion(pred[]{:T(512)S(6)} %eq.11, f32[1,1,2,13824]{3,2,1,0:T(2,128)} %param.3), kind=kLoop, calls=%fused_computation.16 | loop fusion | flops 27648 | bytes 221185 | tf_op jit(solution)/shard_map/jit(_where)/select_n | solution.py:98
  8.9 1.3 %slice_reduce_fusion.1 = (f32[13824]{0:T(1024)S(1)}, f32[13824]{0:T(1024)S(1)}) fusion(f32[1,2,13824]{2,1,0:T(2,128)} %bitcast.81), kind=kLoop, calls=%fused_computation.19 | loop fusion | bytes 221184 | tf_op jit(solution)/shard_map/slice | solution.py:75
  10.2 0.8 dynamic-slice_subtract_fusion
  12.3 1.3 %add_multiply_fusion = (f32[24]{0:T(128)S(1)}, f32[24]{0:T(128)S(1)}) fusion(f32[]{:T(128)} %bitcast.13, f32[]{:T(128)} %bitcast.12), kind=kLoop, calls=%fused_computation.53 | loop fusion | flops 312 | bytes 200 | tf_op jit(solution)/shard_map/integer_pow | solution.py:42
  14.2 50.6 %all-reduce.2.cloned.1.call-done = f32[1,2,13824]{2,1,0:T(2,128)} async-done(((f32[1,2,13824]{2,1,0:T(2,128)}), f32[1,2,13824]{2,1,0:T(2,128)}) %all-reduce.2.cloned.1.call-update) | async-done | bytes 110608 | tf_op jit(solution)/shard_map/psum | solution.py:99
  64.8 1.5 %collective-permute-start = (f32[1,2,13824]{2,1,0:T(2,128)}, f32[1,2,13824]{2,1,0:T(2,128)S(1)}, u32[]{:S(2)}, u32[]{:S(2)}) collective-permute-start(f32[1,2,13824]{2,1,0:T(2,128)} %all-reduce.2.cloned.1.call-done), channel_id=1, source_target_pairs={{0,1},{1,2},{2,3},{3,0},{4,5},{5,6},{6,7},{7,4},{8,9},{9,10},{10,1... | collective-permute-start | bytes 331784 | tf_op jit(solution)/shard_map/ppermute | solution.py:20
  66.3 4.3 %collective-permute-done = f32[1,2,13824]{2,1,0:T(2,128)S(1)} collective-permute-done((f32[1,2,13824]{2,1,0:T(2,128)}, f32[1,2,13824]{2,1,0:T(2,128)S(1)}, u32[]{:S(2)}, u32[]{:S(2)}) %collective-permute-start) | collective-permute-done | bytes 110624 | tf_op jit(solution)/shard_map/ppermute | solution.py:20
  71.3 2.4 %collective-permute-start.2 = (f32[1,2,13824]{2,1,0:T(2,128)}, f32[1,2,13824]{2,1,0:T(2,128)S(1)}, u32[]{:S(2)}, u32[]{:S(2)}) collective-permute-start(f32[1,2,13824]{2,1,0:T(2,128)} %all-reduce.2.cloned.1.call-done), channel_id=1, source_target_pairs={{0,3},{1,0},{2,1},{3,2},{4,7},{5,4},{6,5},{7,6},{8,11},{9,8},{10,9... | collective-permute-start | bytes 331784 | tf_op jit(solution)/shard_map/ppermute | solution.py:22
  73.7 2.6 %collective-permute-done.1 = f32[1,2,13824]{2,1,0:T(2,128)S(1)} collective-permute-done((f32[1,2,13824]{2,1,0:T(2,128)S(1)}, f32[1,2,13824]{2,1,0:T(2,128)S(1)}, u32[]{:S(2)}, u32[]{:S(2)}) %collective-permute-start.1) | collective-permute-done | bytes 110624 | tf_op jit(solution)/shard_map/ppermute | solution.py:20
  76.3 0.9 constant_dynamic-update-slice_fusion.5
  77.6 0.9 constant_dynamic-update-slice_fusion.1
  79.4 1.4 %maximum_reduce_fusion = f32[4,2,13824]{2,1,0:T(2,128)S(1)} fusion(f32[4,1,1,13824]{3,1,2,0:T(1,128)S(1)} %get-tuple-element.10, f32[4,1,1,13824]{3,1,2,0:T(1,128)S(1)} %get-tuple-element.9), kind=kLoop, calls=%fused_computation.7 | loop fusion | flops 110592 | bytes 884736 | tf_op jit(solution)/shard_map/stack | solution.py:79
  81.8 0.9 reshape.181
  82.7 2.2 %copy.4 = f32[4,2,24,24,24]{4,3,2,1,0:T(8,128)} copy(f32[4,2,24,24,24]{3,2,4,1,0:T(8,128)S(1)} %bitcast.74) | data formatting | bytes 884736 | tf_op jit(solution)/shard_map/transpose | solution.py:64
  84.9 2.2 %reshape.182 = f32[4,48,576]{2,1,0:T(8,128)S(1)} reshape(f32[4,2,24,24,24]{4,3,2,1,0:T(8,128)} %copy.4) | data formatting | bytes 884736 | tf_op jit(solution)/shard_map/reshape | solution.py:65
  87.7 0.9 reshape.183
  88.6 2.0 %copy.5 = f32[4,2,24,24,24]{4,3,2,1,0:T(8,128)} copy(f32[4,2,24,24,24]{3,2,4,1,0:T(8,128)S(1)} %bitcast.75) | data formatting | bytes 884736 | tf_op jit(solution)/shard_map/transpose | solution.py:64
  90.6 2.2 %reshape.184 = f32[4,48,576]{2,1,0:T(8,128)S(1)} reshape(f32[4,2,24,24,24]{4,3,2,1,0:T(8,128)} %copy.5) | data formatting | bytes 884736 | tf_op jit(solution)/shard_map/reshape | solution.py:65
  93.5 0.9 reshape.185
  94.3 2.0 %copy.6 = f32[4,2,24,24,24]{4,3,2,1,0:T(8,128)} copy(f32[4,2,24,24,24]{3,2,4,1,0:T(8,128)S(1)} %bitcast.76) | data formatting | bytes 884736 | tf_op jit(solution)/shard_map/transpose | solution.py:64
  96.3 2.2 %reshape_reshape.7 = f32[4,48,576]{2,1,0:T(8,128)S(1)} reshape(f32[4,2,24,24,24]{4,3,2,1,0:T(8,128)} %copy.6) | data formatting | bytes 884736 | tf_op jit(solution)/shard_map/reshape;reshape | solution.py:67
  99.2 0.9 reshape.186
  100.1 2.0 %copy.7 = f32[4,2,24,24,24]{4,3,2,1,0:T(8,128)} copy(f32[4,2,24,24,24]{3,2,4,1,0:T(8,128)S(1)} %bitcast.77) | data formatting | bytes 884736 | tf_op jit(solution)/shard_map/transpose | solution.py:64
  102.1 2.2 %reshape.187 = f32[4,48,576]{2,1,0:T(8,128)S(1)} reshape(f32[4,2,24,24,24]{4,3,2,1,0:T(8,128)} %copy.7) | data formatting | bytes 884736 | tf_op jit(solution)/shard_map/reshape | solution.py:65
  104.9 0.9 reshape.188
  105.8 2.0 %copy.8 = f32[4,2,24,24,24]{4,3,2,1,0:T(8,128)} copy(f32[4,2,24,24,24]{3,2,4,1,0:T(8,128)S(1)} %bitcast.78) | data formatting | bytes 884736 | tf_op jit(solution)/shard_map/transpose | solution.py:64
  107.8 2.5 %reshape.189 = f32[4,48,576]{2,1,0:T(8,128)S(1)} reshape(f32[4,2,24,24,24]{4,3,2,1,0:T(8,128)} %copy.8) | data formatting | bytes 884736 | tf_op jit(solution)/shard_map/reshape | solution.py:65
  110.9 0.9 reshape.190
  111.7 2.0 %copy.9 = f32[4,2,24,24,24]{4,3,2,1,0:T(8,128)} copy(f32[4,2,24,24,24]{3,2,4,1,0:T(8,128)S(1)} %bitcast.79) | data formatting | bytes 884736 | tf_op jit(solution)/shard_map/transpose | solution.py:64
  113.7 3.4 %reshape_reshape_reshape.3 = f32[4,1,2,13824]{3,1,2,0:T(1,128)S(1)} reshape(f32[4,2,24,24,24]{4,3,2,1,0:T(8,128)} %copy.9) | data formatting | bytes 884736 | tf_op jit(solution)/shard_map/reshape;reshape;reshape | solution.py:81
  117.1 0.9 subtract_reduce_fusion
  118.2 0.7 maximum_bitcast_fusion
  (39 shorter events, 7.9 us)
Async XLA Ops:
  6.5 58.3 %all-reduce.2.cloned.1.call-start = ((), (), s32[]{:S(2)}) async-start(), calls=%async_computation | async-start | bytes 221184 | tf_op jit(solution)/shard_map/psum | solution.py:99
  64.8 5.9 %collective-permute-start = (f32[1,2,13824]{2,1,0:T(2,128)}, f32[1,2,13824]{2,1,0:T(2,128)S(1)}, u32[]{:S(2)}, u32[]{:S(2)}) collective-permute-start(f32[1,2,13824]{2,1,0:T(2,128)} %all-reduce.2.cloned.1.call-done), channel_id=1, source_target_pairs={{0,1},{1,2},{2,3},{3,0},{4,5},{5,6},{6,7},{7,4},{8,9},{9,10},{10,1... | collective-permute-start | bytes 331784 | tf_op jit(solution)/shard_map/ppermute | solution.py:20
  70.6 5.6 %collective-permute-start.1 = (f32[1,2,13824]{2,1,0:T(2,128)S(1)}, f32[1,2,13824]{2,1,0:T(2,128)S(1)}, u32[]{:S(2)}, u32[]{:S(2)}) collective-permute-start(f32[1,2,13824]{2,1,0:T(2,128)S(1)} %collective-permute-done), channel_id=1, source_target_pairs={{0,1},{1,2},{2,3},{3,0},{4,5},{5,6},{6,7},{7,4},{8,9},{9,10},{10,1... | collective-permute-start | bytes 331784 | tf_op jit(solution)/shard_map/ppermute | solution.py:20
  71.3 6.2 %collective-permute-start.2 = (f32[1,2,13824]{2,1,0:T(2,128)}, f32[1,2,13824]{2,1,0:T(2,128)S(1)}, u32[]{:S(2)}, u32[]{:S(2)}) collective-permute-start(f32[1,2,13824]{2,1,0:T(2,128)} %all-reduce.2.cloned.1.call-done), channel_id=1, source_target_pairs={{0,3},{1,0},{2,1},{3,2},{4,7},{5,4},{6,5},{7,6},{8,11},{9,8},{10,9... | collective-permute-start | bytes 331784 | tf_op jit(solution)/shard_map/ppermute | solution.py:22
  78.5 0.9 copy-start
  113.7 3.4 %copy-start.1 = (f32[8,2,13824]{2,1,0:T(2,128)S(1)}, f32[8,2,13824]{2,1,0:T(2,128)}, u32[]{:S(2)}) copy-start(f32[8,2,13824]{2,1,0:T(2,128)} %copy-done) | copy-start | bytes 2654212
Sparse Core Ops, SparseCore 0:
  9.7 55.0 all-reduce.1
